TPU v7x, 256 devices: a whole 4x4x8 slice. The times are simulated.
256 devices in a mesh: mp: 32 (over z, y_hi, core), dp: 8 (over x, y_lo).
Axes of the slice: x: 4, y: 4 (y_hi: 2, y_lo: 2; y = y_hi * 2 + y_lo), z: 8, core: 2. Of those that a mesh axis runs over, the one named last changes fastest.
Arguments:
- tokens: bfloat16 [1024, 8192], P('mp', 'dp'), may hold values from -6 to 6
- gate_weight: bfloat16 [8192, 16384], P('dp', 'mp'), may hold values from -0.0625 to 0.0625
- up_weight: bfloat16 [8192, 16384], P('dp', 'mp'), may hold values from -0.0625 to 0.0625
- down_weight: bfloat16 [16384, 8192], P('mp', 'dp'), may hold values from -0.046875 to 0.046875
- cotangent: bfloat16 [1024, 8192], P('mp', 'dp'), may hold values from -6 to 6
Outputs:
- mixed: bfloat16 [1024, 8192], P('mp', 'dp')
- token_grad: bfloat16 [1024, 8192], P('mp', 'dp')
- gate_grad: bfloat16 [8192, 16384], P('dp', 'mp')
- up_grad: bfloat16 [8192, 16384], P('dp', 'mp')
- down_grad: bfloat16 [16384, 8192], P('mp', 'dp')
All inputs are finite; a program needn't handle non-finite values.
Results may differ from a plain program's by a relative error of at most 0.005.
Values may be sent and summed in bfloat16 or wider, within the bound.
No kernel may reach another device: no remote copies, remote signals or barrier semaphores. Data moves between devices by JAX's collectives and lax.ppermute only.
A program may use at most 64 MiB of HBM per device.

v0:
```python
import jax
import jax.numpy as jnp
from jax import lax
from jax.sharding import PartitionSpec as P


def contract_rows(left, right):
    return lax.dot_general(
        left, right, (((0,), (0,)), ((), ())), preferred_element_type=jnp.float32
    )


def contract_cols(left, right):
    return lax.dot_general(
        left, right, (((1,), (1,)), ((), ())), preferred_element_type=jnp.float32
    )


def body(tokens, gate_weight, up_weight, down_weight, cotangent):
    token_all = lax.all_gather(tokens, "mp", axis=0, tiled=True)
    width = gate_weight.shape[1]
    block = token_all
    first = jnp.dot(block, gate_weight, preferred_element_type=jnp.float32)
    second = jnp.dot(block, up_weight, preferred_element_type=jnp.float32)
    both = lax.psum(jnp.concatenate([first, second], axis=1), "dp")
    gate = both[:, :width]
    up = both[:, width:]
    sig = jax.nn.sigmoid(gate)
    act = gate * sig
    hidden_part = (act * up).astype(jnp.bfloat16)
    block = hidden_part
    mixed = lax.psum_scatter(
        jnp.dot(block, down_weight, preferred_element_type=jnp.float32),
        "mp",
        scatter_dimension=0,
        tiled=True,
    ).astype(jnp.bfloat16)
    cot_all = lax.all_gather(cotangent, "mp", axis=0, tiled=True)
    down_grad = contract_rows(hidden_part, cot_all).astype(jnp.bfloat16)
    block = cot_all
    hidden_back = lax.psum(contract_cols(block, down_weight), "dp")
    pre_gate = (hidden_back * up * sig * (1.0 + gate * (1.0 - sig))).astype(jnp.bfloat16)
    pre_up = (hidden_back * act).astype(jnp.bfloat16)
    gate_all, up_all = (pre_gate, pre_up)
    gate_grad = contract_rows(token_all, gate_all).astype(jnp.bfloat16)
    up_grad = contract_rows(token_all, up_all).astype(jnp.bfloat16)
    first = gate_all
    second = up_all
    token_grad = lax.psum_scatter(
        contract_cols(first, gate_weight) + contract_cols(second, up_weight),
        "mp",
        scatter_dimension=0,
        tiled=True,
    ).astype(jnp.bfloat16)
    return (mixed, token_grad, gate_grad, up_grad, down_grad)


def solution(mesh):
    in_specs = (P("mp", "dp"), P("dp", "mp"), P("dp", "mp"), P("mp", "dp"), P("mp", "dp"))
    out_specs = (P("mp", "dp"), P("mp", "dp"), P("dp", "mp"), P("dp", "mp"), P("mp", "dp"))
    return jax.shard_map(body, mesh=mesh, in_specs=in_specs, out_specs=out_specs, check_vma=False)
```

profile of v0, /device:TPU:6, one launch (start us, length us, event | category | flops | bytes accessed | tf_op | source)
XLA Modules:
  0.0 717.8 jit_solution(3119205423730051404)
XLA Ops:
  7.2 0.0 copy-start
  7.2 0.0 all-gather.3.cloned.1.call-start
  7.2 0.7 all-gather.3.cloned.1.call-update
  7.9 0.0 all-gather.5.cloned.1.call-start
  8.0 0.7 all-gather.5.cloned.1.call-update
  8.7 0.0 all-reduce.3.cloned.1.call-start
  8.7 84.9 %all-gather.3.cloned.1.call-done = bf16[1024,1024]{1,0:T(8,128)(2,1)} async-done(((bf16[32,1024]{1,0:T(8,128)(2,1)}), bf16[1024,1024]{1,0:T(8,128)(2,1)}) %all-gather.3.cloned.1.call-update) | async-done | bytes 2097168 | tf_op jit(solution)/shard_map/all_gather | solution.py:20
  93.6 3.3 fusion.4
  96.9 1.3 fusion.3
  98.2 2.5 pad_maximum_fusion
  100.7 72.0 %all-gather.5.cloned.1.call-done = bf16[1024,1024]{1,0:T(8,128)(2,1)} async-done(((bf16[32,1024]{1,0:T(8,128)(2,1)}), bf16[1024,1024]{1,0:T(8,128)(2,1)}) %all-gather.5.cloned.1.call-update) | async-done | bytes 2097168 | tf_op jit(solution)/shard_map/all_gather | solution.py:38
  172.7 4.2 fusion.6
  176.9 0.0 all-reduce.3.cloned.1.call-update
  176.9 0.0 reduce-scatter.5.cloned.1.call-start
  177.0 262.9 %all-reduce.3.cloned.1.call-done = (f32[1024,1024]{0,1:T(8,128)}, f32[1024,512]{0,1:T(8,128)}) async-done(((f32[1024,1024]{0,1:T(8,128)}, f32[1024,512]{0,1:T(8,128)}), (f32[1024,1024]{0,1:T(8,128)}, f32[1024,512]{0,1:T(8,128)})) %all-reduce.3.cloned.1.call-update) | async-done | bytes 6291472 | tf_op jit(solution)/shard_map/psum | solution.py:25
  439.9 4.3 multiply_convert_fusion
  444.2 1.3 fusion.7
  445.5 0.3 copy-done.1
  445.8 3.3 convolution_add_fusion
  449.1 0.0 reduce-scatter.5.cloned.1.call-update
  449.1 0.2 reduce-scatter.3.cloned.1.call-start
  449.3 4.5 fusion.5
  453.8 0.0 reduce-scatter.3.cloned.1.call-update
  453.8 4.1 fusion.1
  458.0 2.3 copy.11
  460.3 3.8 fusion.2
  464.1 2.3 copy.12
  466.4 3.9 convolution_convert_fusion
  470.2 109.2 %reduce-scatter.5.cloned.1.call-done = f32[32,1024]{1,0:T(8,128)} async-done(((f32[1024,1024]{1,0:T(8,128)}), f32[32,1024]{1,0:T(8,128)}) %reduce-scatter.5.cloned.1.call-update) | async-done | bytes 131088 | tf_op jit(solution)/shard_map/reduce_scatter | solution.py:49
  579.4 1.5 convert_element_type.34
  581.0 128.8 %reduce-scatter.3.cloned.1.call-done = f32[32,1024]{1,0:T(8,128)} async-done(((f32[1024,1024]{1,0:T(8,128)}), f32[32,1024]{1,0:T(8,128)}) %reduce-scatter.3.cloned.1.call-update) | async-done | bytes 131088 | tf_op jit(solution)/shard_map/reduce_scatter | solution.py:32
  709.8 1.5 convert_element_type.31
  (8 shorter events, 0.0 us)
Async XLA Ops:
  7.2 89.7 %copy-start = (bf16[1024,512]{1,0:T(8,128)(2,1)S(1)}, bf16[1024,512]{1,0:T(8,128)(2,1)}, u32[]{:S(2)}) copy-start(bf16[1024,512]{1,0:T(8,128)(2,1)} %param.6) | copy-start | bytes 3145732
  7.2 86.4 %all-gather.3.cloned.1.call-start = ((), (), s32[]{:S(2)}) async-start(), calls=%async_computation.2 | async-start | bytes 2162688 | tf_op jit(solution)/shard_map/all_gather | solution.py:20
  7.9 164.8 %all-gather.5.cloned.1.call-start = ((), (), s32[]{:S(2)}) async-start(), calls=%async_computation.4 | async-start | bytes 2162688 | tf_op jit(solution)/shard_map/all_gather | solution.py:38
  8.7 431.2 %all-reduce.3.cloned.1.call-start = ((), (), s32[]{:S(2)}) async-start(), calls=%async_computation.6 | async-start | bytes 12582912 | tf_op jit(solution)/shard_map/psum | solution.py:25
  93.6 3.3 copy-start.4
  98.2 74.5 %copy-start.3 = (bf16[512,1024]{1,0:T(8,128)(2,1)S(1)}, bf16[512,1024]{1,0:T(8,128)(2,1)}, u32[]{:S(2)}) copy-start(bf16[512,1024]{1,0:T(8,128)(2,1)} %param.8) | copy-start | bytes 3145732
  176.9 402.5 %reduce-scatter.5.cloned.1.call-start = ((), (), s32[]{:S(2)}) async-start(), calls=%async_computation.5 | async-start | bytes 4325376 | tf_op jit(solution)/shard_map/reduce_scatter | solution.py:49
  444.2 1.3 copy-start.2
  444.2 1.6 copy-start.1
  449.1 260.7 %reduce-scatter.3.cloned.1.call-start = ((), (), s32[]{:S(2)}) async-start(), calls=%async_computation.3 | async-start | bytes 4325376 | tf_op jit(solution)/shard_map/reduce_scatter | solution.py:32
Sparse Core Ops, SparseCore 0:
  10.8 82.7 all-gather.2
  96.4 76.3 all-gather.4
  177.1 262.8 all-reduce.2
  449.2 130.1 reduce-scatter.4
  583.5 126.2 reduce-scatter.2
where the time goes:
time: 718 us
  waiting for transfers between devices  659 us (92%)
  matrix products  29.7 us (4%)
  between operations  13.9 us (2%)
  other arithmetic  9.84 us (1%)
    psum x1, waiting for transfers between devices, body(): both = lax.psum(jnp.concatenate([first, second], axis=1), 'dp')  263 us
    reduce_scatter x1, waiting for transfers between devices, body(): lax.psum_scatter(jnp.dot(block, down_weight, preferred_element_type=jnp.f...  129 us
    reduce_scatter x1, waiting for transfers between devices, body(): lax.psum_scatter(contract_cols(first, gate_weight) + contract_cols(second...  109 us
    all_gather x1, waiting for transfers between devices, body(): token_all = lax.all_gather(tokens, 'mp', axis=0, tiled=True)  84.9 us
    all_gather x1, waiting for transfers between devices, body(): cot_all = lax.all_gather(cotangent, 'mp', axis=0, tiled=True)  72 us
  transfers between devices with their start and end apart: 5, of which 5 were waited for; matrix products, arithmetic and copies ran while one was open for 4% of the time, Pallas kernels for 0%

commit v1 on v0

--- a/solution.py
+++ b/solution.py
@@ -17,7 +17,9 @@
 
 
 def body(tokens, gate_weight, up_weight, down_weight, cotangent):
-    token_all = lax.all_gather(tokens, "mp", axis=0, tiled=True)
+    token_all = jnp.concatenate(
+        lax.all_to_all(jnp.stack([tokens] * lax.axis_size("mp")), "mp", 0, 0), axis=0
+    )
     width = gate_weight.shape[1]
     block = token_all
     first = jnp.dot(block, gate_weight, preferred_element_type=jnp.float32)

time: 718 us -> 658 us (0.916)
  waiting for transfers between devices: 659 us -> 585 us
  starting transfers between devices: 0.38 us -> 11.8 us
    all_gather x1 -> x0, waiting for transfers between devices: 84.9 us -> none  [body(): token_all = lax.all_gather(tokens, 'mp', axis=0, tiled=True)]
    all_to_all x0 -> x1, waiting for transfers between devices: none -> 52 us  [body(): lax.all_to_all(jnp.stack([tokens] * lax.axis_size('mp')), 'mp', 0, 0)]
    all_gather x1, waiting for transfers between devices: 72 us -> 31.1 us  [body(): cot_all = lax.all_gather(cotangent, 'mp', axis=0, tiled=True)]
    all_to_all x0 -> x1, starting transfers between devices: none -> 11.5 us  [body(): lax.all_to_all(jnp.stack([tokens] * lax.axis_size('mp')), 'mp', 0, 0)]
where the time goes in v1:
time: 658 us; the launch traced here: 657 us
  waiting for transfers between devices  585 us (89%)
  matrix products  29.7 us (5%)
  between operations  13.9 us (2%)
  starting transfers between devices  11.8 us (2%)
  other arithmetic  9.84 us (1%)
  local copies, waits for them, and re-layouts  7.38 us (1%)
    psum x1, waiting for transfers between devices, body(): both = lax.psum(jnp.concatenate([first, second], axis=1), 'dp')  263 us
    reduce_scatter x1, waiting for transfers between devices, body(): lax.psum_scatter(jnp.dot(block, down_weight, preferred_element_type=jnp.f...  129 us
    reduce_scatter x1, waiting for transfers between devices, body(): lax.psum_scatter(contract_cols(first, gate_weight) + contract_cols(second...  109 us
    all_to_all x1, waiting for transfers between devices, body(): lax.all_to_all(jnp.stack([tokens] * lax.axis_size('mp')), 'mp', 0, 0)  52 us
    all_gather x1, waiting for transfers between devices, body(): cot_all = lax.all_gather(cotangent, 'mp', axis=0, tiled=True)  31.1 us
  transfers between devices with their start and end apart: 5, of which 5 were waited for; matrix products, arithmetic and copies ran while one was open for 4% of the time, Pallas kernels for 0%

profile of v1, /device:TPU:6, one launch (start us, length us, event | category | flops | bytes accessed | tf_op | source)
XLA Modules:
  0.0 657.3 jit_solution(4397207195503864926)
XLA Ops:
  7.2 0.0 copy-start
  7.2 2.5 stack.2
  9.7 11.5 %all-to-all-start = ((bf16[32,32,1024]{2,1,0:T(8,128)(2,1)}), bf16[32,32,1024]{2,1,0:T(8,128)(2,1)S(1)}, u32[]{:S(2)}, u32[]{:S(2)}) async-start(bf16[32,32,1024]{2,1,0:T(8,128)(2,1)} %stack.2), calls=%async_computation | async-start | bytes 4194304 | tf_op jit(solution)/shard_map/all_to_all | solution.py:21
  21.2 0.0 all-gather.2.cloned.1.call-start
  21.2 0.7 all-gather.2.cloned.1.call-update
  21.9 0.0 all-reduce.3.cloned.1.call-start
  22.0 52.0 %all-to-all-done = bf16[32,32,1024]{2,1,0:T(8,128)(2,1)S(1)} async-done(((bf16[32,32,1024]{2,1,0:T(8,128)(2,1)}), bf16[32,32,1024]{2,1,0:T(8,128)(2,1)S(1)}, u32[]{:S(2)}, u32[]{:S(2)}) %all-to-all-start) | async-done | bytes 2097184 | tf_op jit(solution)/shard_map/all_to_all | solution.py:21
  74.0 3.3 fusion.4
  77.3 1.3 fusion.3
  78.6 2.5 pad_maximum_fusion
  81.1 31.1 %all-gather.2.cloned.1.call-done = bf16[1024,1024]{1,0:T(8,128)(2,1)} async-done(((bf16[32,1024]{1,0:T(8,128)(2,1)}), bf16[1024,1024]{1,0:T(8,128)(2,1)}) %all-gather.2.cloned.1.call-update) | async-done | bytes 2097168 | tf_op jit(solution)/shard_map/all_gather | solution.py:40
  112.2 4.2 fusion.6
  116.4 0.0 all-reduce.3.cloned.1.call-update
  116.4 0.0 reduce-scatter.5.cloned.1.call-start
  116.4 262.9 %all-reduce.3.cloned.1.call-done = (f32[1024,1024]{0,1:T(8,128)}, f32[1024,512]{0,1:T(8,128)}) async-done(((f32[1024,1024]{0,1:T(8,128)}, f32[1024,512]{0,1:T(8,128)}), (f32[1024,1024]{0,1:T(8,128)}, f32[1024,512]{0,1:T(8,128)})) %all-reduce.3.cloned.1.call-update) | async-done | bytes 6291472 | tf_op jit(solution)/shard_map/psum | solution.py:27
  379.4 4.3 multiply_convert_fusion
  383.6 1.3 fusion.7
  385.0 0.3 copy-done.2
  385.2 3.3 convolution_add_fusion
  388.5 0.0 reduce-scatter.5.cloned.1.call-update
  388.6 0.2 reduce-scatter.3.cloned.1.call-start
  388.8 4.5 fusion.5
  393.3 0.0 reduce-scatter.3.cloned.1.call-update
  393.3 4.1 fusion.1
  397.4 2.3 copy.11
  399.7 3.8 fusion.2
  403.5 2.3 copy.12
  405.8 3.9 convolution_convert_fusion
  409.7 109.2 %reduce-scatter.5.cloned.1.call-done = f32[32,1024]{1,0:T(8,128)} async-done(((f32[1024,1024]{1,0:T(8,128)}), f32[32,1024]{1,0:T(8,128)}) %reduce-scatter.5.cloned.1.call-update) | async-done | bytes 131088 | tf_op jit(solution)/shard_map/reduce_scatter | solution.py:51
  518.9 1.5 convert_element_type.34
  520.4 128.8 %reduce-scatter.3.cloned.1.call-done = f32[32,1024]{1,0:T(8,128)} async-done(((f32[1024,1024]{1,0:T(8,128)}), f32[32,1024]{1,0:T(8,128)}) %reduce-scatter.3.cloned.1.call-update) | async-done | bytes 131088 | tf_op jit(solution)/shard_map/reduce_scatter | solution.py:34
  649.2 1.5 convert_element_type.31
  (8 shorter events, 0.0 us)
Async XLA Ops:
  7.2 70.1 %copy-start = (bf16[1024,512]{1,0:T(8,128)(2,1)S(1)}, bf16[1024,512]{1,0:T(8,128)(2,1)}, u32[]{:S(2)}) copy-start(bf16[1024,512]{1,0:T(8,128)(2,1)} %param.6) | copy-start | bytes 3145732
  9.7 64.3 %all-to-all-start = ((bf16[32,32,1024]{2,1,0:T(8,128)(2,1)}), bf16[32,32,1024]{2,1,0:T(8,128)(2,1)S(1)}, u32[]{:S(2)}, u32[]{:S(2)}) async-start(bf16[32,32,1024]{2,1,0:T(8,128)(2,1)} %stack.2), calls=%async_computation | async-start | bytes 4194304 | tf_op jit(solution)/shard_map/all_to_all | solution.py:21
  21.2 91.0 %all-gather.2.cloned.1.call-start = ((), (), s32[]{:S(2)}) async-start(), calls=%async_computation.4 | async-start | bytes 2162688 | tf_op jit(solution)/shard_map/all_gather | solution.py:40
  21.9 357.4 %all-reduce.3.cloned.1.call-start = ((), (), s32[]{:S(2)}) async-start(), calls=%async_computation.6 | async-start | bytes 12582912 | tf_op jit(solution)/shard_map/psum | solution.py:27
  74.0 3.3 copy-start.1
  78.6 33.6 %copy-start.4 = (bf16[512,1024]{1,0:T(8,128)(2,1)S(1)}, bf16[512,1024]{1,0:T(8,128)(2,1)}, u32[]{:S(2)}) copy-start(bf16[512,1024]{1,0:T(8,128)(2,1)} %param.8) | copy-start | bytes 3145732
  116.4 402.5 %reduce-scatter.5.cloned.1.call-start = ((), (), s32[]{:S(2)}) async-start(), calls=%async_computation.5 | async-start | bytes 4325376 | tf_op jit(solution)/shard_map/reduce_scatter | solution.py:51
  383.6 1.3 copy-start.3
  383.6 1.6 copy-start.2
  388.6 260.6 %reduce-scatter.3.cloned.1.call-start = ((), (), s32[]{:S(2)}) async-start(), calls=%async_computation.3 | async-start | bytes 4325376 | tf_op jit(solution)/shard_map/reduce_scatter | solution.py:34
Sparse Core Ops, SparseCore 0:
  24.8 87.3 all-gather.1
  116.5 262.7 all-reduce.2
  388.7 130.1 reduce-scatter.4
  523.0 126.1 reduce-scatter.2
